TPU v7x, 256 devices: a whole 4x4x8 slice. The times are simulated.
256 devices in a mesh: row: 16 (over x, z_lo), col: 16 (over z_hi, y, core).
Axes of the slice: x: 4, y: 4, z: 8 (z_hi: 2, z_lo: 4; z = z_hi * 4 + z_lo), core: 2. Of those that a mesh axis runs over, the one named last changes fastest.
Arguments:
- tensor: float32 [32, 2048, 4096], P(None, 'row', 'col'), may hold values from -6 to 6
- initial_first: float32 [2048, 256], P('row'), may hold values from -6 to 6
- initial_second: float32 [4096, 256], P('col'), may hold values from -6 to 6
Outputs:
- factor_first: float32 [2048, 256], P('row')
- factor_second: float32 [4096, 256], P('col')
- factor_frames: float32 [32, 256], replicated
- weights: float32 [256], replicated
All inputs are finite; a program needn't handle non-finite values.
Results may differ from a plain program's by a relative error of at most 0.00024.
Values sent between devices are 32-bit elements; how exact they have to be, the bound alone decides.
No kernel may reach another device: no remote copies, remote signals or barrier semaphores. Data moves between devices by JAX's collectives and lax.ppermute only.
A program may use at most 128 MiB of HBM per device.

v0:
```python
import math
import jax
import jax.numpy as jnp
from jax import lax
from jax.sharding import PartitionSpec as P

PASSES = 2
epsilon = 1e-06


def solve_gram(partials, hadamard):
    factor_lower = jnp.linalg.cholesky(hadamard)
    midway = lax.linalg.triangular_solve(
        factor_lower, partials, left_side=False, lower=True, transpose_a=True
    )
    return lax.linalg.triangular_solve(
        factor_lower, midway, left_side=False, lower=True, transpose_a=False
    )


def local_gram(matrix):
    return jnp.dot(matrix.T, matrix, precision=lax.Precision.HIGHEST)


def normalize_second(unscaled, row_count):
    squares = lax.psum(jnp.sum(unscaled * unscaled, axis=0), "col")
    scaling = jnp.sqrt(squares / row_count + epsilon)
    normed = unscaled / scaling
    gram_new = lax.psum(local_gram(normed), "col") / row_count
    return (normed, gram_new)


def body(tensor, initial_first, initial_second):
    highest = lax.Precision.HIGHEST
    frames = tensor.shape[0]
    rows_first = tensor.shape[1] * lax.axis_size("row")
    rows_second = tensor.shape[2] * lax.axis_size("col")
    first_gram = lax.psum(local_gram(initial_first), "row") / rows_first
    second = initial_second
    second_gram = lax.psum(local_gram(initial_second), "col") / rows_second
    contracted = jnp.einsum("kij,ir->kjr", tensor, initial_first, precision=highest)
    for repeat in range(PASSES):
        frame_terms = jnp.einsum("kjr,jr->kr", contracted, second, precision=highest)
        frame_sums = lax.psum(frame_terms, ("row", "col"))
        frame_raw = solve_gram(frame_sums, first_gram * second_gram) / math.sqrt(
            rows_first * rows_second
        )
        frame_scaling = jnp.sqrt(jnp.mean(frame_raw * frame_raw, axis=0) + epsilon)
        factor_frames = frame_raw / frame_scaling
        frame_gram = local_gram(factor_frames) / frames
        second_terms = jnp.einsum("kjr,kr->jr", contracted, factor_frames, precision=highest)
        hadamard = first_gram * frame_gram
        second_sums = lax.psum(second_terms, "row")
        second_raw = solve_gram(second_sums, hadamard) / math.sqrt(rows_first * frames)
        second, second_gram = normalize_second(second_raw, rows_second)
    second_contracted = jnp.einsum("kij,jr->kir", tensor, second, precision=highest)
    first_terms = jnp.einsum("kir,kr->ir", second_contracted, factor_frames, precision=highest)
    hadamard = second_gram * frame_gram
    first_sums = lax.psum(first_terms, "col")
    first_raw = solve_gram(first_sums, hadamard) / math.sqrt(rows_second * frames)
    squares = lax.psum(jnp.sum(first_raw * first_raw, axis=0), "row")
    weights = jnp.sqrt(squares / rows_first + epsilon)
    factor_first = first_raw / weights
    return (factor_first, second, factor_frames, weights)


def solution(mesh):
    placed = (P(None, "row", "col"), P("row", None), P("col", None))
    return jax.shard_map(
        body,
        mesh=mesh,
        in_specs=placed,
        out_specs=(P("row", None), P("col", None), P(), P()),
        check_vma=False,
    )
```

profile of v0, /device:TPU:0, one launch (start us, length us, event | category | flops | bytes accessed | tf_op | source)
XLA Modules:
  0.0 1450.2 jit_solution(4500966303370641703)
XLA Ops:
  9.3 2.3 fusion.91
  11.7 10.7 multiply_reduce_fusion.2
  22.5 10.3 copy.41
  32.8 80.0 %psum.86 = f32[32,256]{0,1:T(8,128)S(1)} all-reduce(f32[32,256]{0,1:T(8,128)S(1)} %bitcast.271), channel_id=1, replica_groups=mesh['row'=16,'col'=16] {'row','col'}, use_global_device_ids=true, to_apply=%region_6.0 | all-reduce | flops 8192 | bytes 65536 | tf_op jit(solution)/shard_map/psum | solution.py:44
  112.9 58.9 %all-reduce.9.cloned.1.call-done = f32[256,256]{0,1:T(8,128)} async-done(((f32[256,256]{0,1:T(8,128)}), f32[256,256]{0,1:T(8,128)}) %all-reduce.9.cloned.1.call-update) | async-done | bytes 262160 | tf_op jit(solution)/shard_map/psum | solution.py:38
  171.8 178.5 %all-reduce.11.cloned.1.call-done = f32[256,256]{0,1:T(8,128)} async-done(((f32[256,256]{0,1:T(8,128)}), f32[256,256]{0,1:T(8,128)}) %all-reduce.11.cloned.1.call-update) | async-done | bytes 262160 | tf_op jit(solution)/shard_map/psum | solution.py:40
  351.5 11.7 cholesky.256
  363.3 9.8 custom-call.34
  373.6 11.7 cholesky.273
  387.4 4.0 while.18
  388.0 1.4 bitcast_dynamic-update-slice_fusion.11
  390.0 1.4 bitcast_dynamic-update-slice_fusion.11
  391.4 19.9 %custom-call.35 = f32[2,128,128]{1,2,0:T(8,128)S(1)} custom-call(f32[2,128,128]{2,1,0:T(8,128)S(1)} %get-tuple-element.73), custom_call_target="InvertDiagBlocksLowerTriangular" | custom-call | tf_op jit(solution)/shard_map/triangular_solve/custom-call.0 | solution.py:13
  414.3 11.7 cholesky.290
  426.1 9.8 custom-call.37
  436.4 11.7 cholesky.307
  449.4 4.1 multiply_reduce_fusion.1
  456.2 4.0 while.19
  460.2 19.7 %custom-call.38 = f32[2,128,128]{1,2,0:T(8,128)S(1)} custom-call(f32[2,128,128]{2,1,0:T(8,128)S(1)} %get-tuple-element.75), custom_call_target="InvertDiagBlocksLowerTriangular" | custom-call | tf_op jit(solution)/shard_map/triangular_solve/custom-call.5 | solution.py:13
  479.9 135.7 %all-reduce.13.cloned.1.call-done = f32[256,256]{0,1:T(8,128)} async-done(((f32[256,256]{0,1:T(8,128)}), f32[256,256]{0,1:T(8,128)}) %all-reduce.13.cloned.1.call-update) | async-done | bytes 262160 | tf_op jit(solution)/shard_map/psum | solution.py:53
  619.3 42.8 %psum.88 = f32[256]{0:T(256)S(1)} all-reduce(f32[256]{0:T(256)S(1)} %multiply_reduce_fusion.4), channel_id=1, replica_groups=mesh['row'=16,'col'=16] {'col'}, use_global_device_ids=true, to_apply=%region_10.16 | all-reduce | flops 256 | bytes 2048 | tf_op jit(solution)/shard_map/psum | solution.py:26
  663.5 9.3 fusion.11
  672.8 76.3 %psum.90 = f32[32,256]{0,1:T(8,128)S(1)} all-reduce(f32[32,256]{0,1:T(8,128)S(1)} %bitcast.269), channel_id=1, replica_groups=mesh['row'=16,'col'=16] {'row','col'}, use_global_device_ids=true, to_apply=%region_12.18 | all-reduce | flops 8192 | bytes 65536 | tf_op jit(solution)/shard_map/psum | solution.py:44
  749.1 87.1 %all-reduce.15.cloned.1.call-done = f32[256,256]{0,1:T(8,128)} async-done(((f32[256,256]{0,1:T(8,128)}), f32[256,256]{0,1:T(8,128)}) %all-reduce.15.cloned.1.call-update) | async-done | bytes 262160 | tf_op jit(solution)/shard_map/psum | solution.py:29
  837.4 11.7 cholesky.324
  849.2 9.8 custom-call.40
  859.5 11.7 cholesky.341
  873.8 4.0 while.20
  877.9 20.1 %custom-call.41 = f32[2,128,128]{1,2,0:T(8,128)S(1)} custom-call(f32[2,128,128]{2,1,0:T(8,128)S(1)} %get-tuple-element.77), custom_call_target="InvertDiagBlocksLowerTriangular" | custom-call | tf_op jit(solution)/shard_map/triangular_solve/custom-call.0 | solution.py:13
  900.0 11.7 cholesky.358
  911.8 9.8 custom-call.43
  922.1 11.7 cholesky.375
  935.1 4.2 multiply_reduce_fusion
  941.6 4.0 while.21
  945.5 19.7 %custom-call.44 = f32[2,128,128]{1,2,0:T(8,128)S(1)} custom-call(f32[2,128,128]{2,1,0:T(8,128)S(1)} %get-tuple-element.79), custom_call_target="InvertDiagBlocksLowerTriangular" | custom-call | tf_op jit(solution)/shard_map/triangular_solve/custom-call.5 | solution.py:13
  965.3 135.7 %all-reduce.17.cloned.1.call-done = f32[256,256]{0,1:T(8,128)} async-done(((f32[256,256]{0,1:T(8,128)}), f32[256,256]{0,1:T(8,128)}) %all-reduce.17.cloned.1.call-update) | async-done | bytes 262160 | tf_op jit(solution)/shard_map/psum | solution.py:53
  1104.7 42.8 %psum.92 = f32[256]{0:T(256)S(1)} all-reduce(f32[256]{0:T(256)S(1)} %multiply_reduce_fusion.3), channel_id=1, replica_groups=mesh['row'=16,'col'=16] {'col'}, use_global_device_ids=true, to_apply=%region_16.22 | all-reduce | flops 256 | bytes 2048 | tf_op jit(solution)/shard_map/psum | solution.py:26
  1147.6 5.5 fusion.5
  1154.3 6.3 fusion
  1161.4 172.7 %all-reduce.19.cloned.1.call-done = (f32[128,256]{0,1:T(8,128)}, f32[256,256]{0,1:T(8,128)}) async-done(((f32[128,256]{0,1:T(8,128)}, f32[256,256]{0,1:T(8,128)}), (f32[128,256]{0,1:T(8,128)}, f32[256,256]{0,1:T(8,128)})) %all-reduce.19.cloned.1.call-update) | async-done | bytes 393232 | tf_op jit(solution)/shard_map/psum | solution.py:59
  1335.3 11.7 cholesky.392
  1347.1 10.0 custom-call.46
  1357.6 11.7 cholesky.409
  1372.1 4.1 while.17
  1372.7 1.4 bitcast_dynamic-update-slice_fusion.10
  1374.7 1.4 bitcast_dynamic-update-slice_fusion.10
  1376.2 19.7 %custom-call.25 = f32[2,128,128]{1,2,0:T(8,128)S(1)} custom-call(f32[2,128,128]{2,1,0:T(8,128)S(1)} %get-tuple-element.48), custom_call_target="InvertDiagBlocksLowerTriangular" | custom-call | tf_op jit(solution)/shard_map/triangular_solve | solution.py:13
  1399.3 42.9 %psum.95 = f32[256]{0:T(256)S(1)} all-reduce(f32[256]{0:T(256)S(1)} %multiply_reduce_fusion.5), channel_id=1, replica_groups=mesh['row'=16,'col'=16] {'row'}, use_global_device_ids=true, to_apply=%region_20.26 | all-reduce | flops 256 | bytes 2048 | tf_op jit(solution)/shard_map/psum | solution.py:61
  (166 shorter events, 51.2 us)
Async XLA Ops:
  7.2 0.9 copy-start
  7.2 164.6 %all-reduce.9.cloned.1.call-start = ((), (), s32[]{:S(2)}) async-start(), calls=%async_computation | async-start | bytes 524288 | tf_op jit(solution)/shard_map/psum | solution.py:38
  9.2 341.0 %all-reduce.11.cloned.1.call-start = ((), (), s32[]{:S(2)}) async-start(), calls=%async_computation.1 | async-start | bytes 524288 | tf_op jit(solution)/shard_map/psum | solution.py:40
  11.6 604.0 %all-reduce.13.cloned.1.call-start = ((), (), s32[]{:S(2)}) async-start(), calls=%async_computation.2 | async-start | bytes 524288 | tf_op jit(solution)/shard_map/psum | solution.py:53
  453.6 382.7 %copy-start.1 = (f32[256,256]{0,1:T(8,128)S(1)}, f32[256,256]{0,1:T(8,128)}, u32[]{:S(2)}) copy-start(f32[256,256]{0,1:T(8,128)} %all-reduce.9.cloned.1.call-done) | copy-start | bytes 786436
  454.8 381.4 %all-reduce.15.cloned.1.call-start = ((), (), s32[]{:S(2)}) async-start(), calls=%async_computation.3 | async-start | bytes 524288 | tf_op jit(solution)/shard_map/psum | solution.py:29
  663.4 437.6 %all-reduce.17.cloned.1.call-start = ((), (), s32[]{:S(2)}) async-start(), calls=%async_computation.4 | async-start | bytes 524288 | tf_op jit(solution)/shard_map/psum | solution.py:53
  899.4 205.2 %copy-start.2 = (f32[32,256]{1,0:T(8,128)}, f32[32,256]{1,0:T(8,128)S(1)}, u32[]{:S(2)}) copy-start(f32[32,256]{1,0:T(8,128)S(1)} %fusion.76) | copy-start | bytes 98308
  940.2 393.9 %all-reduce.19.cloned.1.call-start = ((), (), s32[]{:S(2)}) async-start(), calls=%async_computation.5 | async-start | bytes 786432 | tf_op jit(solution)/shard_map/psum | solution.py:59
  1442.2 0.9 copy-start.3
Sparse Core Ops, SparseCore 0:
  10.6 161.1 all-reduce.8
  175.2 175.0 all-reduce.10
  454.9 160.5 all-reduce.12
  663.5 172.6 all-reduce.14
  940.4 160.5 all-reduce.16
  1160.7 173.3 all-reduce.18
where the time goes:
time: 1460 us; the launch traced here: 1450 us
  waiting for transfers between devices  769 us (53%)
  blocking collectives  285 us (20%)
  other arithmetic  284 us (19%)
  matrix products  54.8 us (4%)
  local copies, waits for them, and re-layouts  35.9 us (2%)
  between operations  21.6 us (1%)
    psum x2, waiting for transfers between devices, body(): second_sums = lax.psum(second_terms, 'row')  271 us
    psum x1, waiting for transfers between devices, body(): second_gram = lax.psum(local_gram(initial_second), 'col') / rows_second  178 us
    psum x1, waiting for transfers between devices, body(): first_sums = lax.psum(first_terms, 'col')  173 us
    another operation x34, other arithmetic, solve_gram(): factor_lower = jnp.linalg.cholesky(hadamard)  173 us
    psum x2, blocking collectives, body(): frame_sums = lax.psum(frame_terms, ('row', 'col'))  156 us
    another operation x11, other arithmetic, solve_gram(): lax.linalg.triangular_solve(factor_lower, partials, left_side=False, lowe...  99.1 us
    psum x1, waiting for transfers between devices, normalize_second(): gram_new = lax.psum(local_gram(normed), 'col') / row_count  87.1 us
    psum x2, blocking collectives, normalize_second(): squares = lax.psum(jnp.sum(unscaled * unscaled, axis=0), 'col')  85.5 us
  transfers between devices with their start and end apart: 6, of which 6 were waited for; matrix products, arithmetic and copies ran while one was open for 6% of the time, Pallas kernels for 0%

commit v1 on v0

--- a/solution.py
+++ b/solution.py
@@ -26,7 +26,7 @@
     squares = lax.psum(jnp.sum(unscaled * unscaled, axis=0), "col")
     scaling = jnp.sqrt(squares / row_count + epsilon)
     normed = unscaled / scaling
-    gram_new = lax.psum(local_gram(normed), "col") / row_count
+    gram_new = jnp.sum(lax.all_gather(local_gram(normed), "col"), axis=0) / row_count
     return (normed, gram_new)
 
 

time: 1460 us -> 1380 us (0.945)
  waiting for transfers between devices: 769 us -> 686 us
    psum x1 -> x0, waiting for transfers between devices: 87.1 us -> none  [normalize_second(): gram_new = lax.psum(local_gram(normed), 'col') / row_count]
    psum x1, waiting for transfers between devices: 173 us -> 111 us  [body(): first_sums = lax.psum(first_terms, 'col')]
    all_gather x0 -> x2, waiting for transfers between devices: none -> 60.8 us  [normalize_second(): lax.all_gather(local_gram(normed), 'col')]
  transfers between devices with their start and end apart: 6 -> 7, of which waited for: 6 -> 6; matrix products, arithmetic and copies ran while one was open for 6% -> 11% of each run, Pallas kernels for 0% -> 0%
where the time goes in v1:
time: 1380 us
  waiting for transfers between devices  686 us (50%)
  blocking collectives  293 us (21%)
  other arithmetic  287 us (21%)
  matrix products  53.9 us (4%)
  local copies, waits for them, and re-layouts  36.1 us (3%)
  between operations  21.5 us (2%)
    psum x2, waiting for transfers between devices, body(): second_sums = lax.psum(second_terms, 'row')  267 us
    psum x1, waiting for transfers between devices, body(): second_gram = lax.psum(local_gram(initial_second), 'col') / rows_second  178 us
    another operation x34, other arithmetic, solve_gram(): factor_lower = jnp.linalg.cholesky(hadamard)  172 us
    psum x2, blocking collectives, body(): frame_sums = lax.psum(frame_terms, ('row', 'col'))  164 us
    psum x1, waiting for transfers between devices, body(): first_sums = lax.psum(first_terms, 'col')  111 us
    another operation x11, other arithmetic, solve_gram(): lax.linalg.triangular_solve(factor_lower, partials, left_side=False, lowe...  99.1 us
    psum x2, blocking collectives, normalize_second(): squares = lax.psum(jnp.sum(unscaled * unscaled, axis=0), 'col')  85.5 us
    psum x1, waiting for transfers between devices, body(): first_gram = lax.psum(local_gram(initial_first), 'row') / rows_first  68.7 us
  transfers between devices with their start and end apart: 7, of which 6 were waited for; matrix products, arithmetic and copies ran while one was open for 11% of the time, Pallas kernels for 0%

profile of v1, /device:TPU:0, one launch (start us, length us, event | category | flops | bytes accessed | tf_op | source)
XLA Modules:
  0.0 1377.9 jit_solution(22259913116173968)
XLA Ops:
  9.3 2.4 fusion.91
  11.7 10.7 multiply_reduce_fusion.2
  22.5 80.5 %psum.72 = f32[32,256]{0,1:T(8,128)S(1)} all-reduce(f32[32,256]{0,1:T(8,128)S(1)} %bitcast.275), channel_id=1, replica_groups=mesh['row'=16,'col'=16] {'row','col'}, use_global_device_ids=true, to_apply=%region_6.0 | all-reduce | flops 8192 | bytes 65536 | tf_op jit(solution)/shard_map/psum | solution.py:44
  103.0 68.7 %all-reduce.7.cloned.1.call-done = f32[256,256]{0,1:T(8,128)} async-done(((f32[256,256]{0,1:T(8,128)}), f32[256,256]{0,1:T(8,128)}) %all-reduce.7.cloned.1.call-update) | async-done | bytes 262160 | tf_op jit(solution)/shard_map/psum | solution.py:38
  171.8 178.3 %all-reduce.9.cloned.1.call-done = f32[256,256]{0,1:T(8,128)} async-done(((f32[256,256]{0,1:T(8,128)}), f32[256,256]{0,1:T(8,128)}) %all-reduce.9.cloned.1.call-update) | async-done | bytes 262160 | tf_op jit(solution)/shard_map/psum | solution.py:40
  351.3 11.7 cholesky.256
  363.1 9.8 custom-call.34
  373.4 11.7 cholesky.273
  387.2 4.0 while.18
  387.8 1.4 bitcast_dynamic-update-slice_fusion.11
  389.8 1.4 bitcast_dynamic-update-slice_fusion.11
  391.2 19.9 %custom-call.35 = f32[2,128,128]{1,2,0:T(8,128)S(1)} custom-call(f32[2,128,128]{2,1,0:T(8,128)S(1)} %get-tuple-element.73), custom_call_target="InvertDiagBlocksLowerTriangular" | custom-call | tf_op jit(solution)/shard_map/triangular_solve/custom-call.0 | solution.py:13
  413.2 11.7 cholesky.290
  424.9 9.8 custom-call.37
  435.2 11.7 cholesky.307
  448.3 4.1 multiply_reduce_fusion.1
  455.1 4.0 while.19
  459.1 19.7 %custom-call.38 = f32[2,128,128]{1,2,0:T(8,128)S(1)} custom-call(f32[2,128,128]{2,1,0:T(8,128)S(1)} %get-tuple-element.75), custom_call_target="InvertDiagBlocksLowerTriangular" | custom-call | tf_op jit(solution)/shard_map/triangular_solve/custom-call.5 | solution.py:13
  478.8 135.7 %all-reduce.11.cloned.1.call-done = f32[256,256]{0,1:T(8,128)} async-done(((f32[256,256]{0,1:T(8,128)}), f32[256,256]{0,1:T(8,128)}) %all-reduce.11.cloned.1.call-update) | async-done | bytes 262160 | tf_op jit(solution)/shard_map/psum | solution.py:53
  618.2 42.8 %psum.74 = f32[256]{0:T(256)S(1)} all-reduce(f32[256]{0:T(256)S(1)} %multiply_reduce_fusion.4), channel_id=1, replica_groups=mesh['row'=16,'col'=16] {'col'}, use_global_device_ids=true, to_apply=%region_10.16 | all-reduce | flops 256 | bytes 2048 | tf_op jit(solution)/shard_map/psum | solution.py:26
  662.2 10.3 copy.52
  672.6 9.4 fusion.11
  682.0 83.5 %psum.75 = f32[32,256]{0,1:T(8,128)S(1)} all-reduce(f32[32,256]{0,1:T(8,128)S(1)} %bitcast.273), channel_id=1, replica_groups=mesh['row'=16,'col'=16] {'row','col'}, use_global_device_ids=true, to_apply=%region_12.18 | all-reduce | flops 8192 | bytes 65536 | tf_op jit(solution)/shard_map/psum | solution.py:44
  765.5 2.5 reduce_sum.65
  768.4 11.7 cholesky.324
  780.1 9.8 custom-call.40
  790.4 11.7 cholesky.341
  804.8 4.0 while.20
  808.8 20.1 %custom-call.41 = f32[2,128,128]{1,2,0:T(8,128)S(1)} custom-call(f32[2,128,128]{2,1,0:T(8,128)S(1)} %get-tuple-element.77), custom_call_target="InvertDiagBlocksLowerTriangular" | custom-call | tf_op jit(solution)/shard_map/triangular_solve/custom-call.0 | solution.py:13
  831.0 11.7 cholesky.358
  842.7 9.8 custom-call.43
  853.0 11.7 cholesky.375
  866.0 4.1 multiply_reduce_fusion
  872.5 4.0 while.21
  876.5 19.7 %custom-call.44 = f32[2,128,128]{1,2,0:T(8,128)S(1)} custom-call(f32[2,128,128]{2,1,0:T(8,128)S(1)} %get-tuple-element.79), custom_call_target="InvertDiagBlocksLowerTriangular" | custom-call | tf_op jit(solution)/shard_map/triangular_solve/custom-call.5 | solution.py:13
  896.2 131.7 %all-reduce.13.cloned.1.call-done = f32[256,256]{0,1:T(8,128)} async-done(((f32[256,256]{0,1:T(8,128)}), f32[256,256]{0,1:T(8,128)}) %all-reduce.13.cloned.1.call-update) | async-done | bytes 262160 | tf_op jit(solution)/shard_map/psum | solution.py:53
  1031.6 42.8 %psum.77 = f32[256]{0:T(256)S(1)} all-reduce(f32[256]{0:T(256)S(1)} %multiply_reduce_fusion.3), channel_id=1, replica_groups=mesh['row'=16,'col'=16] {'col'}, use_global_device_ids=true, to_apply=%region_16.22 | all-reduce | flops 256 | bytes 2048 | tf_op jit(solution)/shard_map/psum | solution.py:26
  1076.6 5.5 fusion.5
  1082.2 6.3 fusion
  1088.5 60.8 %all-gather.7.cloned.1.call-done = f32[4096,256]{1,0:T(8,128)} async-done(((f32[256,256]{1,0:T(8,128)}), f32[4096,256]{1,0:T(8,128)}) %all-gather.7.cloned.1.call-update) | async-done | bytes 4194320 | tf_op jit(solution)/shard_map/all_gather | solution.py:29
  1149.3 2.5 reduce_sum.68
  1152.1 11.7 cholesky.392
  1163.9 10.0 custom-call.46
  1174.4 11.7 cholesky.409
  1188.8 4.1 while.17
  1192.9 19.7 %custom-call.25 = f32[2,128,128]{1,2,0:T(8,128)S(1)} custom-call(f32[2,128,128]{2,1,0:T(8,128)S(1)} %get-tuple-element.48), custom_call_target="InvertDiagBlocksLowerTriangular" | custom-call | tf_op jit(solution)/shard_map/triangular_solve | solution.py:13
  1212.6 111.0 %all-reduce.15.cloned.1.call-done = f32[128,256]{0,1:T(8,128)} async-done(((f32[128,256]{0,1:T(8,128)}), f32[128,256]{0,1:T(8,128)}) %all-reduce.15.cloned.1.call-update) | async-done | bytes 131088 | tf_op jit(solution)/shard_map/psum | solution.py:59
  1327.0 43.0 %psum.79 = f32[256]{0:T(256)S(1)} all-reduce(f32[256]{0:T(256)S(1)} %multiply_reduce_fusion.5), channel_id=1, replica_groups=mesh['row'=16,'col'=16] {'row'}, use_global_device_ids=true, to_apply=%region_20.26 | all-reduce | flops 256 | bytes 2048 | tf_op jit(solution)/shard_map/psum | solution.py:61
  (173 shorter events, 51.5 us)
Async XLA Ops:
  7.2 0.9 copy-start
  7.2 164.6 %all-reduce.7.cloned.1.call-start = ((), (), s32[]{:S(2)}) async-start(), calls=%async_computation | async-start | bytes 524288 | tf_op jit(solution)/shard_map/psum | solution.py:38
  9.2 340.8 %all-reduce.9.cloned.1.call-start = ((), (), s32[]{:S(2)}) async-start(), calls=%async_computation.1 | async-start | bytes 524288 | tf_op jit(solution)/shard_map/psum | solution.py:40
  11.7 602.8 %all-reduce.11.cloned.1.call-start = ((), (), s32[]{:S(2)}) async-start(), calls=%async_computation.2 | async-start | bytes 524288 | tf_op jit(solution)/shard_map/psum | solution.py:53
  171.8 240.8 %copy-start.1 = (f32[256,256]{0,1:T(8,128)S(1)}, f32[256,256]{0,1:T(8,128)}, u32[]{:S(2)}) copy-start(f32[256,256]{0,1:T(8,128)} %all-reduce.7.cloned.1.call-done) | copy-start | bytes 786436
  453.7 311.8 %all-gather.5.cloned.1.call-start = ((), (), s32[]{:S(2)}) async-start(), calls=%async_computation.5 | async-start | bytes 4456448 | tf_op jit(solution)/shard_map/all_gather | solution.py:29
  662.2 365.7 %all-reduce.13.cloned.1.call-start = ((), (), s32[]{:S(2)}) async-start(), calls=%async_computation.3 | async-start | bytes 524288 | tf_op jit(solution)/shard_map/psum | solution.py:53
  830.3 245.4 %copy-start.2 = (f32[32,256]{1,0:T(8,128)}, f32[32,256]{1,0:T(8,128)S(1)}, u32[]{:S(2)}) copy-start(f32[32,256]{1,0:T(8,128)S(1)} %fusion.76) | copy-start | bytes 98308
  871.2 278.1 %all-gather.7.cloned.1.call-start = ((), (), s32[]{:S(2)}) async-start(), calls=%async_computation.6 | async-start | bytes 4456448 | tf_op jit(solution)/shard_map/all_gather | solution.py:29
  1075.6 247.9 %all-reduce.15.cloned.1.call-start = ((), (), s32[]{:S(2)}) async-start(), calls=%async_computation.4 | async-start | bytes 262144 | tf_op jit(solution)/shard_map/psum | solution.py:59
  1370.0 0.9 copy-start.3
Sparse Core Ops, SparseCore 0:
  10.6 161.1 all-reduce.6
  175.1 174.8 all-reduce.8
  453.8 160.5 all-reduce.10
  662.3 73.9 all-gather.4
  871.3 156.5 all-reduce.12
  1075.8 73.4 all-gather.6
  1152.5 171.0 all-reduce.14
